TPU v7x, 32 devices: a whole 2x2x4 slice. The times are simulated.
32 devices in a mesh: grp: 8 (over z, core), col: 4 (over y, x).
Axes of the slice: x: 2, y: 2, z: 4, core: 2. Of those that a mesh axis runs over, the one named last changes fastest.
Arguments:
- constraint_rows: float32 [2048, 16384], P('grp', 'col'), may hold values from -0.1875 to 0.1875
- shift: float32 [16384], P('col'), may hold values from 0.3 to 1
- group_rows: int32 [8], replicated, may hold values from 1 to 256, 1024 in all
- panel_index: int32 [1], replicated, may hold values from 0 to 31
Outputs:
- panel_factor: float32 [16384, 512], P(('col', 'grp'))
Inputs may be any that keep to these rules, and one draw needn't show every extreme that they name: `group_rows`: the values sum to 1024 and the largest equals 256.
All inputs are finite; a program needn't handle non-finite values.
Results may differ from a plain program's by a relative error of at most 0.000076.
Values sent between devices are 32-bit elements; how exact they have to be, the bound alone decides.
No kernel may reach another device: no remote copies, remote signals or barrier semaphores. Data moves between devices by JAX's collectives and lax.ppermute only.
A program may use at most 64 MiB of HBM per device.

v0:
```python
import functools
import jax
import jax.numpy as jnp
from jax import lax
from jax.experimental import pallas as pl
from jax.experimental.pallas import tpu as pltpu
from jax.sharding import PartitionSpec as P

PANEL = 512
BLOCK = 128
LINE = 4
HIGHEST = lax.Precision.HIGHEST
HIGH = lax.Precision.HIGH


def dot(left, right, over_left, over_right, precision=HIGHEST):
    return lax.dot_general(
        left,
        right,
        (((over_left,), (over_right,)), ((), ())),
        precision=precision,
        preferred_element_type=jnp.float32,
    )


def wide(row, like):
    return jnp.broadcast_to(row, like.shape)


def eliminate(tiles, inverse):
    count = len(tiles)
    sub = lax.broadcasted_iota(jnp.int32, tiles[0].shape, 0)
    width = tiles[0].shape[1]
    done = []
    for j in range(count):
        own, inv = tiles[j], inverse[j]
        cols = [wide(own[:, 8 * j + i : 8 * j + i + 1], own) for i in range(8)]
        upper, roots, scale = {}, [], None
        for i in range(8):
            root = lax.rsqrt(wide(cols[i][i : i + 1, :], own))
            roots.append(root)
            scale = root if scale is None else jnp.where(sub >= i, root, scale)
            below = jnp.where(sub > i, cols[i] * root, 0.0)
            for m in range(i + 1, 8):
                upper[i, m] = wide(cols[m][i : i + 1, :], own) * root
                cols[m] = cols[m] - below * upper[i, m]
            own = own - below * (wide(own[i : i + 1, :], own) * root)
            inv = inv - below * (wide(inv[i : i + 1, :], own) * root)
        own, inv = own * scale, inv * scale
        done.append(inv)
        if j + 1 < count:
            nxt, nxt_inv = tiles[j + 1], inverse[j + 1]
            parts = []
            for i in range(8):
                part = wide(nxt[:, 8 * j + i : 8 * j + i + 1], own)
                for q in range(i):
                    part = part - parts[q] * upper[q, i]
                parts.append(part * roots[i])
            for i in range(8):
                nxt = nxt - parts[i] * wide(own[i : i + 1, :], own)
                nxt_inv = nxt_inv - parts[i] * wide(inv[i : i + 1, :], own)
            tiles[j + 1], inverse[j + 1] = nxt, nxt_inv
        if j + 2 < count:
            rest = dot(own, jnp.concatenate([own, inv], 1), 0, 0)
            for t in range(j + 2, count):
                tiles[t] = tiles[t] - rest[8 * t : 8 * t + 8, :width]
                inverse[t] = inverse[t] - rest[8 * t : 8 * t + 8, width:]
    return jnp.concatenate(done, 0)


def invert_step(low, first, a_in, w_in, a_ref, w_ref):
    order = a_in.shape[0]
    high = low + BLOCK
    if first:
        w_ref[...] = jnp.zeros_like(w_ref)
    else:
        w_ref[...] = w_in[...]
    lane = lax.broadcasted_iota(jnp.int32, (8, BLOCK), 1)
    sub = lax.broadcasted_iota(jnp.int32, (8, BLOCK), 0)
    steps = range(0, BLOCK, 8)
    tiles = [a_in[low + t : low + t + 8, low:high] for t in steps]
    inverse = [jnp.where(lane == sub + t, 1.0, 0.0).astype(jnp.float32) for t in steps]
    own = eliminate(tiles, inverse)
    w_ref[low:high, low:high] = own
    if low > 0:
        w_ref[low:high, :low] = dot(own, w_ref[low:high, :low], 1, 0)
    if high < order:
        below = dot(a_in[high:, low:high], own, 1, 1)
        a_ref[high:, high:] = a_in[high:, high:] - dot(below, below, 1, 1)
        w_ref[high:, :high] = w_ref[high:, :high] - dot(below, w_ref[low:high, :high], 1, 0)


def inverse_factor(block):
    order = block.shape[0]
    work, inv = block, block
    shape = jax.ShapeDtypeStruct(block.shape, jnp.float32)
    for low in range(0, order, BLOCK):
        work, inv = pl.pallas_call(
            functools.partial(invert_step, low, low == 0),
            out_shape=(shape, shape),
            compiler_params=pltpu.CompilerParams(vmem_limit_bytes=24 << 20),
            cost_estimate=pl.CostEstimate(flops=order**3, transcendentals=0, bytes_accessed=20 << 20),
            name="invert_step",
        )(work, inv)
    return inv


def add_shift(values, shift_part, first_row, start):
    row_ids = first_row + jnp.arange(values.shape[0], dtype=jnp.int32)
    col_ids = jnp.arange(values.shape[1], dtype=jnp.int32)
    on_diag = row_ids[:, None] == start + col_ids[None, :]
    return values + jnp.where(on_diag, shift_part[:, None], jnp.zeros_like(values))


def spread(value, axis, source):
    kept = jnp.where(lax.axis_index(axis) == source, value, 0).astype(value.dtype)
    return lax.psum(kept, axis)


def general(masked, local, owner, add_own):
    own_cols = lax.dynamic_slice_in_dim(masked, local, PANEL, 1)
    panel_cols = spread(own_cols, "col", owner)
    mine = lax.psum_scatter(dot(masked, panel_cols, 0, 0), "grp", scatter_dimension=0, tiled=True)
    mine = add_own(mine)
    from_owner = spread(mine, "col", owner)
    shard = lax.all_gather(from_owner, "grp", axis=0, tiled=True)
    block = lax.dynamic_slice_in_dim(shard, local, PANEL, 0)
    return dot(mine, inverse_factor(block), 1, 1)


def take_panel(index_ref, count_ref, rows_ref, shift_ref, first_ref, second_ref, held, sem):
    depth, width = held.shape[0], rows_ref.shape[1]
    start = index_ref[0] * PANEL
    owner = start // width
    local = start - owner * width
    mine = lax.axis_index("col") == owner
    limit = jnp.where(mine, count_ref[lax.axis_index("grp")], 0)
    copy = pltpu.make_async_copy(rows_ref.at[:, pl.ds(pl.multiple_of(local, PANEL), PANEL)], held, sem)
    copy.start()
    copy.wait()
    half = PANEL // 2
    live = lax.broadcasted_iota(jnp.int32, (depth, half), 0) < limit
    for side, out in enumerate((first_ref, second_ref)):
        out[:depth, :] = jnp.where(live, held[:, side * half : (side + 1) * half], 0.0)
        for q in range(half // 128):
            line = shift_ref[pl.ds(local // 128 + side * (half // 128) + q, 1), :]
            line = jnp.where(mine, line, 0.0)
            out[depth:, q * 128 : (q + 1) * 128] = jnp.broadcast_to(line, (8, 128))


def panel_halves(rows, shift, group_rows, panel_index):
    depth = rows.shape[0]
    shape = jax.ShapeDtypeStruct((depth + 8, PANEL // 2), jnp.float32)
    smem, vmem = pl.BlockSpec(memory_space=pltpu.SMEM), pl.BlockSpec(memory_space=pltpu.VMEM)
    return pl.pallas_call(
        take_panel,
        out_shape=(shape, shape),
        in_specs=[smem, smem, pl.BlockSpec(memory_space=pl.ANY), vmem],
        out_specs=(vmem, vmem),
        scratch_shapes=[pltpu.VMEM((depth, PANEL), jnp.float32), pltpu.SemaphoreType.DMA(())],
        name="take_panel",
    )(panel_index, group_rows, rows, shift.reshape(-1, 128))


def both_cores(pairs):
    return [(2 * a + core, 2 * b + core) for a, b in pairs for core in (0, 1)]


INWARD = both_cores([(0, 1), (3, 2)])
ACROSS = both_cores([(1, 2), (2, 1)])
OUTWARD = both_cores([(1, 0), (2, 3)])
SIDE = INWARD + OUTWARD


def ordered(low, mine, other, axis):
    return jnp.where(low, jnp.concatenate([mine, other], axis), jnp.concatenate([other, mine], axis))


def hold(first, second, first_in=None, second_in=None):
    if first_in is None:
        return lax.optimization_barrier((first, second))
    first, second, first_in, second_in = lax.optimization_barrier((first, second, first_in, second_in))
    return first + first_in, second + second_in


def on_line(rows, shift, group_rows, panel_index, share, add_own):
    grp, col = lax.axis_index("grp"), lax.axis_index("col")
    z, core = grp // 2, grp % 2
    left = z < 2
    core_pairs = [(g, g ^ 1) for g in range(2 * LINE)]
    x_pairs = [(c, c ^ 1) for c in range(4)]
    y_pairs = [(c, c ^ 2) for c in range(4)]

    first, second = panel_halves(rows, shift, group_rows, panel_index)
    first, second = hold(first, second, lax.ppermute(first, "col", x_pairs), lax.ppermute(second, "col", y_pairs))
    first, second = hold(first, second)
    first, second = hold(first, second, lax.ppermute(first, "col", y_pairs), lax.ppermute(second, "col", x_pairs))
    sent = jnp.concatenate([first, second], 1)
    depth = rows.shape[0]
    panel, diag = sent[:depth], sent[depth]
    panel_other = lax.ppermute(panel, "grp", core_pairs)

    early = lax.dynamic_slice_in_dim(rows, 2 * (z ^ 1) * share, 2 * share, 1)
    early = lax.ppermute(early, "grp", INWARD)
    early_other = lax.dynamic_slice_in_dim(early, (1 - core) * share, share, 1)
    early_other = lax.ppermute(early_other, "grp", core_pairs)
    early = lax.dynamic_slice_in_dim(early, core * share, share, 1)
    quarter = lax.dynamic_slice_in_dim(panel, col * (depth // 4), depth // 4, 0)
    end = lax.ppermute(quarter, "grp", INWARD)
    end = ordered(col % 2 == 0, end, lax.ppermute(end, "col", x_pairs), 0)
    end = ordered(col < 2, end, lax.ppermute(end, "col", y_pairs), 0)
    end_other = lax.ppermute(end, "grp", core_pairs)
    side = dot(early, end, 0, 0, HIGH) + dot(early_other, end_other, 0, 0, HIGH)

    piece = PANEL // 8
    at = (core * 4 + col) * piece
    part = dot(lax.dynamic_slice_in_dim(panel, at, piece, 1), panel, 0, 0) + dot(
        lax.dynamic_slice_in_dim(panel_other, at, piece, 1), panel_other, 0, 0
    )
    part = part + lax.ppermute(part, "grp", SIDE)
    part = part + lax.ppermute(part, "grp", ACROSS)
    outer = lax.ppermute(part, "grp", OUTWARD)
    part = jnp.where((z == 0) | (z == LINE - 1), outer, part)
    part = ordered(col % 2 == 0, part, lax.ppermute(part, "col", x_pairs), 0)
    part = ordered(col < 2, part, lax.ppermute(part, "col", y_pairs), 0)
    block = ordered(core == 0, part, lax.ppermute(part, "grp", core_pairs), 0)
    on_diag = jnp.arange(PANEL)[:, None] == jnp.arange(PANEL)[None, :]
    block = block + jnp.where(on_diag, diag[:, None], 0.0)
    inverse = inverse_factor(block)

    far_end, far_hub = jnp.where(left, 3, 0), jnp.where(left, 2, 1)
    to_end = [0, share // 2 - 8, share]
    to_hub = [0, share // 2 + 16, share]

    def products(chip, cuts):
        here = lax.dynamic_slice_in_dim(rows, (2 * chip + core) * share, share, 1)
        there = lax.dynamic_slice_in_dim(rows, (2 * chip + 1 - core) * share, share, 1)
        there = lax.ppermute(there, "grp", core_pairs)
        return [
            dot(here[:, lo:hi], panel, 0, 0, HIGH) + dot(there[:, lo:hi], panel_other, 0, 0, HIGH)
            for lo, hi in zip(cuts[:-1], cuts[1:])
        ]

    def travel(values, pairs):
        return [lax.ppermute(value, "grp", pairs) for value in values]

    def add(values, others):
        return [v + o for v, o in zip(values, others)]

    for_end = products(far_end, to_end)
    for_hub = products(far_hub, to_hub)
    for_side = products(z ^ 1, to_end)
    (own,) = products(z, [0, share])
    ends = travel(for_end, INWARD)
    hubs = travel(for_hub, INWARD)
    ends = travel(add(for_end, ends), ACROSS)
    hubs = travel(add(for_hub, hubs), ACROSS)
    ends = travel(add(for_side, ends), OUTWARD)
    mine = add_own(own + side) + jnp.concatenate(ends, 0) + jnp.concatenate(hubs, 0)
    return dot(mine, inverse, 1, 1)


def on_device(constraint_rows, shift, group_rows, panel_index):
    width = constraint_rows.shape[1]
    groups, columns = lax.axis_size("grp"), lax.axis_size("col")
    col_idx, grp_idx = lax.axis_index("col"), lax.axis_index("grp")
    share = width // groups
    start = panel_index[0] * PANEL
    owner = start // width
    local = start - owner * width
    live_count = lax.dynamic_index_in_dim(group_rows, grp_idx, keepdims=False)
    live = jnp.arange(constraint_rows.shape[0], dtype=jnp.int32) < live_count

    def add_own(mine):
        shift_part = lax.dynamic_slice_in_dim(shift, grp_idx * share, share, 0)
        return add_shift(mine, shift_part, col_idx * width + grp_idx * share, start)

    if groups == 2 * LINE and columns == 4:
        return on_line(constraint_rows, shift, group_rows, panel_index, share, add_own)
    masked = jnp.where(live[:, None], constraint_rows, jnp.zeros_like(constraint_rows))
    return general(masked, local, owner, add_own)


def solution(mesh):
    placed = (P("grp", "col"), P("col"), P(), P())
    return jax.shard_map(
        on_device, mesh=mesh, in_specs=placed, out_specs=P(("col", "grp"), None), check_vma=False
    )
```

profile of v0, /device:TPU:0, one launch (start us, length us, event | category | flops | bytes accessed | tf_op | source)
XLA Modules:
  0.0 151.9 jit_solution(1032975714311501652)
XLA Ops:
  0.7 2.6 %take_panel.1 = (f32[264,256]{1,0:T(8,128)}, f32[264,256]{1,0:T(8,128)}) custom-call(s32[1]{0:T(128)S(6)} %copy.5.index_ref, s32[8]{0:T(128)} %count_ref.1, f32[256,4096]{1,0:T(8,128)} %rows_ref.1, f32[32,128]{1,0:T(8,128)} %bitcast.25), custom_call_target="tpu_custom_call" | custom-call | tf_op jit(solution)/shard_map/take_panel/pallas_call | solution.py:155
  3.3 3.0 %collective-permute-start = (f32[264,256]{1,0:T(8,128)}, f32[264,256]{1,0:T(8,128)S(1)}, u32[]{:S(2)}, u32[]{:S(2)}) collective-permute-start(f32[264,256]{1,0:T(8,128)} %get-tuple-element.26), channel_id=1, source_target_pairs={{0,1},{1,0},{2,3},{3,2},{4,5},{5,4},{6,7},{7,6},{8,9},{9,8},{10,11... | collective-permute-start | bytes 811016 | tf_op jit(solution)/shard_map/ppermute | solution.py:195
  6.3 1.5 %collective-permute-start.1 = (f32[264,256]{1,0:T(8,128)}, f32[264,256]{1,0:T(8,128)S(1)}, u32[]{:S(2)}, u32[]{:S(2)}) collective-permute-start(f32[264,256]{1,0:T(8,128)} %get-tuple-element.28), channel_id=1, source_target_pairs={{0,2},{1,3},{2,0},{3,1},{4,6},{5,7},{6,4},{7,5},{8,10},{9,11},{10,... | collective-permute-start | bytes 811016 | tf_op jit(solution)/shard_map/ppermute | solution.py:195
  7.8 5.2 %collective-permute-done = f32[264,256]{1,0:T(8,128)S(1)} collective-permute-done((f32[264,256]{1,0:T(8,128)}, f32[264,256]{1,0:T(8,128)S(1)}, u32[]{:S(2)}, u32[]{:S(2)}) %collective-permute-start) | collective-permute-done | bytes 270368 | tf_op jit(solution)/shard_map/ppermute | solution.py:195
  13.0 1.5 collective-permute-done.1
  14.5 1.0 add.185
  15.5 1.0 add.184
  16.4 1.6 %collective-permute-start.2 = (f32[264,256]{1,0:T(8,128)S(1)}, f32[264,256]{1,0:T(8,128)S(1)}, u32[]{:S(2)}, u32[]{:S(2)}) collective-permute-start(f32[264,256]{1,0:T(8,128)S(1)} %add.184), channel_id=1, source_target_pairs={{0,2},{1,3},{2,0},{3,1},{4,6},{5,7},{6,4},{7,5},{8,10},{9,11},{10,... | collective-permute-start | bytes 811016 | tf_op jit(solution)/shard_map/ppermute | solution.py:197
  18.6 2.9 %constant_dynamic-slice_fusion = (f32[256,512]{1,0:T(8,128)}, f32[256,512]{1,0:T(8,128)}, f32[256,512]{1,0:T(8,128)}, f32[256,512]{1,0:T(8,128)}) fusion(f32[256,4096]{1,0:T(8,128)} %rows_ref.1, s32[]{:T(128)S(6)} %select_n.137, s32[]{:T(128)S(6)} %select_n.134, s32[]{:T(128)S(6)} %select_n.131, s32[]{:T(128)S(6)} %select_n.118), kind=kLoop, calls=%fused_computation.55 | loop fusion | bytes 4194320 | tf_op jit(solution)/shard_map/dynamic_slice | solution.py:237
  22.0 1.3 constant_dynamic-slice_fusion.5
  23.3 3.5 %collective-permute-start.6 = (f32[256,1024]{1,0:T(8,128)S(1)}, f32[256,1024]{1,0:T(8,128)S(1)}, u32[]{:S(2)}, u32[]{:S(2)}) collective-permute-start(f32[256,1024]{1,0:T(8,128)S(1)} %constant_dynamic-slice_fusion.5), channel_id=1, source_target_pairs={{0,8},{4,12},{24,16},{28,20},{1,9},{5,13},{25,17},{29,21},{2,10},{... | collective-permute-start | bytes 3145736 | tf_op jit(solution)/shard_map/ppermute | solution.py:204
  27.7 1.0 add.187
  28.9 1.7 %fusion.12 = f32[272,512]{1,0:T(8,128)S(1)} fusion(f32[256,512]{1,0:T(8,128)S(1)} %fusion.7, f32[256,4096]{1,0:T(8,128)} %rows_ref.1, s32[]{:T(128)S(6)} %select_n.136), kind=kOutput, calls=%fused_computation.27 | convolution fusion | flops 213909504 | bytes 1474564 | tf_op jit(solution)/shard_map/dot_general | solution.py:17
  30.6 1.5 fusion.24
  32.1 1.5 fusion.27
  33.7 1.8 %fusion.15 = f32[264,512]{1,0:T(8,128)S(1)} fusion(f32[256,512]{1,0:T(8,128)S(1)} %fusion.7, f32[256,4096]{1,0:T(8,128)} %rows_ref.1, s32[]{:T(128)S(6)} %add.238), kind=kOutput, calls=%fused_computation.30 | convolution fusion | flops 207618048 | bytes 1458180 | tf_op jit(solution)/shard_map/dot_general | solution.py:17
  35.4 1.7 %fusion.18 = f32[264,512]{1,0:T(8,128)S(1)} fusion(f32[256,512]{1,0:T(8,128)S(1)} %fusion.7, f32[256,4096]{1,0:T(8,128)} %rows_ref.1, s32[]{:T(128)S(6)} %add.237), kind=kOutput, calls=%fused_computation.33 | convolution fusion | flops 207618048 | bytes 1458180 | tf_op jit(solution)/shard_map/dot_general | solution.py:17
  37.2 1.3 collective-permute-start.7
  38.5 1.7 %fusion.9 = f32[512,512]{1,0:T(8,128)S(1)} fusion(f32[256,512]{1,0:T(8,128)S(1)} %fusion.7, f32[256,4096]{1,0:T(8,128)} %rows_ref.1, s32[]{:T(128)S(6)} %select_n.117), kind=kOutput, calls=%fused_computation.24 | convolution fusion | flops 402653184 | bytes 2097156 | tf_op jit(solution)/shard_map/dot_general | solution.py:17
  40.1 1.5 fusion.21
  41.7 10.5 %collective-permute-done.7 = f32[64,512]{1,0:T(8,128)S(1)} collective-permute-done((f32[64,512]{1,0:T(8,128)S(1)}, f32[64,512]{1,0:T(8,128)S(1)}, u32[]{:S(2)}, u32[]{:S(2)}) %collective-permute-start.7) | collective-permute-done | bytes 131104 | tf_op jit(solution)/shard_map/ppermute | solution.py:209
  52.1 1.5 collective-permute-start.8
  54.1 3.0 %collective-permute-done.8 = f32[64,512]{1,0:T(8,128)S(1)} collective-permute-done((f32[64,512]{1,0:T(8,128)S(1)}, f32[64,512]{1,0:T(8,128)S(1)}, u32[]{:S(2)}, u32[]{:S(2)}) %collective-permute-start.8) | collective-permute-done | bytes 131104 | tf_op jit(solution)/shard_map/ppermute | solution.py:210
  57.6 2.5 %collective-permute-start.25 = (f32[64,512]{1,0:T(8,128)S(1)}, f32[64,512]{1,0:T(8,128)S(1)}, u32[]{:S(2)}, u32[]{:S(2)}) collective-permute-start(f32[64,512]{1,0:T(8,128)S(1)} %convolution_add_fusion.8), channel_id=1, source_target_pairs={{0,8},{4,12},{24,16},{28,20},{8,0},{12,4},{16,24},{20,28},{1,9},{5... | collective-permute-start | bytes 393224 | tf_op jit(solution)/shard_map/ppermute | solution.py:220
  60.2 1.4 convolution_add_fusion.5
  61.5 2.0 %collective-permute-start.14 = (f32[248,512]{1,0:T(8,128)S(1)}, f32[248,512]{1,0:T(8,128)S(1)}, u32[]{:S(2)}, u32[]{:S(2)}) collective-permute-start(f32[248,512]{1,0:T(8,128)S(1)} %convolution_add_fusion.5), channel_id=1, source_target_pairs={{0,8},{4,12},{24,16},{28,20},{1,9},{5,13},{25,17},{29,21},{2,10},{... | collective-permute-start | bytes 1523720 | tf_op jit(solution)/shard_map/ppermute | solution.py:245
  63.5 0.8 collective-permute-done.25
  65.0 1.6 %convolution_add_fusion.3 = f32[264,512]{1,0:T(8,128)S(1)} fusion(f32[264,512]{1,0:T(8,128)S(1)} %fusion.15, f32[256,512]{1,0:T(8,128)S(1)} %collective-permute-done.5, f32[256,512]{1,0:T(8,128)} %collective-permute-done.13), kind=kOutput, calls=%fused_computation.7 | convolution fusion | flops 207753216 | bytes 1998848 | tf_op jit(solution)/shard_map/dot_general | solution.py:17
  67.3 1.3 collective-permute-start.27
  69.1 8.7 %collective-permute-done.27 = f32[64,512]{1,0:T(8,128)S(1)} collective-permute-done((f32[64,512]{1,0:T(8,128)S(1)}, f32[64,512]{1,0:T(8,128)S(1)}, u32[]{:S(2)}, u32[]{:S(2)}) %collective-permute-start.27) | collective-permute-done | bytes 131104 | tf_op jit(solution)/shard_map/ppermute | solution.py:222
  77.8 1.5 collective-permute-start.17
  79.4 1.3 collective-permute-start.23
  80.7 1.6 %collective-permute-start.28 = (f32[64,512]{1,0:T(8,128)S(1)}, f32[64,512]{1,0:T(8,128)S(1)}, u32[]{:S(2)}, u32[]{:S(2)}) collective-permute-start(f32[64,512]{1,0:T(8,128)S(1)} %broadcast_select_fusion), channel_id=1, source_target_pairs={{0,1},{1,0},{2,3},{3,2},{4,5},{5,4},{6,7},{7,6},{8,9},{9,8},{10,11... | collective-permute-start | bytes 393224 | tf_op jit(solution)/shard_map/ppermute | solution.py:224
  82.8 2.9 %collective-permute-done.28 = f32[64,512]{1,0:T(8,128)S(1)} collective-permute-done((f32[64,512]{1,0:T(8,128)S(1)}, f32[64,512]{1,0:T(8,128)S(1)}, u32[]{:S(2)}, u32[]{:S(2)}) %collective-permute-start.28) | collective-permute-done | bytes 131104 | tf_op jit(solution)/shard_map/ppermute | solution.py:224
  85.7 1.3 collective-permute-start.21
  87.2 4.7 %collective-permute-done.17 = f32[264,512]{1,0:T(8,128)S(1)} collective-permute-done((f32[264,512]{1,0:T(8,128)S(1)}, f32[264,512]{1,0:T(8,128)S(1)}, u32[]{:S(2)}, u32[]{:S(2)}) %collective-permute-start.17) | collective-permute-done | bytes 540704 | tf_op jit(solution)/shard_map/ppermute | solution.py:245
  92.7 1.6 %collective-permute-start.29 = (f32[128,512]{1,0:T(8,128)S(1)}, f32[128,512]{1,0:T(8,128)S(1)}, u32[]{:S(2)}, u32[]{:S(2)}) collective-permute-start(f32[128,512]{1,0:T(8,128)S(1)} %maximum_select_fusion.4), channel_id=1, source_target_pairs={{0,2},{1,3},{2,0},{3,1},{4,6},{5,7},{6,4},{7,5},{8,10},{9,11},{10,... | collective-permute-start | bytes 786440 | tf_op jit(solution)/shard_map/ppermute | solution.py:225
  94.3 8.1 %collective-permute-done.23 = f32[240,512]{1,0:T(8,128)S(1)} collective-permute-done((f32[240,512]{1,0:T(8,128)S(1)}, f32[240,512]{1,0:T(8,128)S(1)}, u32[]{:S(2)}, u32[]{:S(2)}) %collective-permute-start.23) | collective-permute-done | bytes 491552 | tf_op jit(solution)/shard_map/ppermute | solution.py:245
  103.9 7.4 %collective-permute-done.21 = f32[272,512]{1,0:T(8,128)S(1)} collective-permute-done((f32[272,512]{1,0:T(8,128)S(1)}, f32[272,512]{1,0:T(8,128)S(1)}, u32[]{:S(2)}, u32[]{:S(2)}) %collective-permute-start.21) | collective-permute-done | bytes 557088 | tf_op jit(solution)/shard_map/ppermute | solution.py:245
  114.7 1.3 collective-permute-start.16
  116.0 1.5 collective-permute-start.19
  118.4 6.5 %invert_step.4 = (f32[512,512]{1,0:T(8,128)S(1)}, f32[512,512]{1,0:T(8,128)S(1)}) custom-call(f32[512,512]{1,0:T(8,128)S(1)} %fusion.6.a_in.w_in, f32[512,512]{1,0:T(8,128)S(1)} %fusion.6.a_in.w_in), custom_call_target="tpu_custom_call" | custom-call | flops 134217728 | bytes 20971520 | tf_op jit(solution)/shard_map/invert_step/pallas_call | solution.py:98
  124.9 6.4 %invert_step.5 = (f32[512,512]{1,0:T(8,128)S(1)}, f32[512,512]{1,0:T(8,128)S(1)}) custom-call(f32[512,512]{1,0:T(8,128)S(1)} %get-tuple-element.36.a_in, f32[512,512]{1,0:T(8,128)S(1)} %get-tuple-element.37.w_in), custom_call_target="tpu_custom_call" | custom-call | flops 134217728 | bytes 20971520 | tf_op jit(solution)/shard_map/invert_step/pallas_call | solution.py:98
  131.3 6.4 %invert_step.6 = (f32[512,512]{1,0:T(8,128)S(1)}, f32[512,512]{1,0:T(8,128)S(1)}) custom-call(f32[512,512]{1,0:T(8,128)S(1)} %get-tuple-element.38.a_in, f32[512,512]{1,0:T(8,128)S(1)} %get-tuple-element.39.w_in), custom_call_target="tpu_custom_call" | custom-call | flops 134217728 | bytes 20971520 | tf_op jit(solution)/shard_map/invert_step/pallas_call | solution.py:98
  137.7 6.2 %invert_step.7 = (f32[512,512]{1,0:T(8,128)}, f32[512,512]{1,0:T(8,128)S(1)}) custom-call(f32[512,512]{1,0:T(8,128)S(1)} %get-tuple-element.40.a_in, f32[512,512]{1,0:T(8,128)S(1)} %get-tuple-element.41.w_in), custom_call_target="tpu_custom_call" | custom-call | flops 134217728 | bytes 20971520 | tf_op jit(solution)/shard_map/invert_step/pallas_call | solution.py:98
  144.0 4.2 %collective-permute-done.19 = f32[264,512]{1,0:T(8,128)S(1)} collective-permute-done((f32[264,512]{1,0:T(8,128)S(1)}, f32[264,512]{1,0:T(8,128)S(1)}, u32[]{:S(2)}, u32[]{:S(2)}) %collective-permute-start.19) | collective-permute-done | bytes 540704 | tf_op jit(solution)/shard_map/ppermute | solution.py:245
  148.2 0.8 fusion.3
  149.1 2.8 %fusion.43 = f32[512,512]{1,0:T(8,128)} fusion(f32[512,512]{1,0:T(8,128)S(1)} %fusion.3, f32[512,512]{1,0:T(8,128)S(1)} %get-tuple-element.42), kind=kOutput, calls=%fused_computation.71 | convolution fusion | flops 1610612736 | bytes 3145728 | tf_op jit(solution)/shard_map/dot_general | solution.py:17
  (66 shorter events, 11.7 us)
Async XLA Ops:
  3.3 9.7 %collective-permute-start = (f32[264,256]{1,0:T(8,128)}, f32[264,256]{1,0:T(8,128)S(1)}, u32[]{:S(2)}, u32[]{:S(2)}) collective-permute-start(f32[264,256]{1,0:T(8,128)} %get-tuple-element.26), channel_id=1, source_target_pairs={{0,1},{1,0},{2,3},{3,2},{4,5},{5,4},{6,7},{7,6},{8,9},{9,8},{10,11... | collective-permute-start | bytes 811016 | tf_op jit(solution)/shard_map/ppermute | solution.py:195
  6.3 8.2 %collective-permute-start.1 = (f32[264,256]{1,0:T(8,128)}, f32[264,256]{1,0:T(8,128)S(1)}, u32[]{:S(2)}, u32[]{:S(2)}) collective-permute-start(f32[264,256]{1,0:T(8,128)} %get-tuple-element.28), channel_id=1, source_target_pairs={{0,2},{1,3},{2,0},{3,1},{4,6},{5,7},{6,4},{7,5},{8,10},{9,11},{10,... | collective-permute-start | bytes 811016 | tf_op jit(solution)/shard_map/ppermute | solution.py:195
  16.4 11.2 %collective-permute-start.2 = (f32[264,256]{1,0:T(8,128)S(1)}, f32[264,256]{1,0:T(8,128)S(1)}, u32[]{:S(2)}, u32[]{:S(2)}) collective-permute-start(f32[264,256]{1,0:T(8,128)S(1)} %add.184), channel_id=1, source_target_pairs={{0,2},{1,3},{2,0},{3,1},{4,6},{5,7},{6,4},{7,5},{8,10},{9,11},{10,... | collective-permute-start | bytes 811016 | tf_op jit(solution)/shard_map/ppermute | solution.py:197
  18.0 9.6 %collective-permute-start.3 = (f32[264,256]{1,0:T(8,128)S(1)}, f32[264,256]{1,0:T(8,128)}, u32[]{:S(2)}, u32[]{:S(2)}) collective-permute-start(f32[264,256]{1,0:T(8,128)S(1)} %add.185), channel_id=1, source_target_pairs={{0,1},{1,0},{2,3},{3,2},{4,5},{5,4},{6,7},{7,6},{8,9},{9,8},{10,11... | collective-permute-start | bytes 811016 | tf_op jit(solution)/shard_map/ppermute | solution.py:197
  21.4 45.9 %collective-permute-start.20 = (f32[256,512]{1,0:T(8,128)}, f32[256,512]{1,0:T(8,128)S(1)}, u32[]{:S(2)}, u32[]{:S(2)}) collective-permute-start(f32[256,512]{1,0:T(8,128)} %get-tuple-element.43), channel_id=1, source_target_pairs={{0,4},{4,0},{8,12},{12,8},{16,20},{20,16},{24,28},{28,24},{1,5},{5... | collective-permute-start | bytes 1572872 | tf_op jit(solution)/shard_map/ppermute | solution.py:238
  21.4 38.7 %collective-permute-start.13 = (f32[256,512]{1,0:T(8,128)}, f32[256,512]{1,0:T(8,128)}, u32[]{:S(2)}, u32[]{:S(2)}) collective-permute-start(f32[256,512]{1,0:T(8,128)} %get-tuple-element.44), channel_id=1, source_target_pairs={{0,4},{4,0},{8,12},{12,8},{16,20},{20,16},{24,28},{28,24},{1,5},{5... | collective-permute-start | bytes 1572872 | tf_op jit(solution)/shard_map/ppermute | solution.py:238
  23.3 56.1 %collective-permute-start.6 = (f32[256,1024]{1,0:T(8,128)S(1)}, f32[256,1024]{1,0:T(8,128)S(1)}, u32[]{:S(2)}, u32[]{:S(2)}) collective-permute-start(f32[256,1024]{1,0:T(8,128)S(1)} %constant_dynamic-slice_fusion.5), channel_id=1, source_target_pairs={{0,8},{4,12},{24,16},{28,20},{1,9},{5,13},{25,17},{29,21},{2,10},{... | collective-permute-start | bytes 3145736 | tf_op jit(solution)/shard_map/ppermute | solution.py:204
  28.8 28.4 %collective-permute-start.5 = (f32[256,512]{1,0:T(8,128)S(1)}, f32[256,512]{1,0:T(8,128)S(1)}, u32[]{:S(2)}, u32[]{:S(2)}) collective-permute-start(f32[256,512]{1,0:T(8,128)S(1)} %fusion.7), channel_id=1, source_target_pairs={{0,4},{4,0},{8,12},{12,8},{16,20},{20,16},{24,28},{28,24},{1,5},{5... | collective-permute-start | bytes 1572872 | tf_op jit(solution)/shard_map/ppermute | solution.py:201
  33.7 23.5 %copy-start.1 = (f32[256,512]{1,0:T(8,128)S(1)}, f32[256,512]{1,0:T(8,128)}, u32[]{:S(2)}) copy-start(f32[256,512]{1,0:T(8,128)} %get-tuple-element.46) | copy-start | bytes 1572868
  37.2 15.0 %collective-permute-start.7 = (f32[64,512]{1,0:T(8,128)S(1)}, f32[64,512]{1,0:T(8,128)S(1)}, u32[]{:S(2)}, u32[]{:S(2)}) collective-permute-start(f32[64,512]{1,0:T(8,128)S(1)} %constant_dynamic-slice_fusion.4), channel_id=1, source_target_pairs={{0,8},{4,12},{24,16},{28,20},{1,9},{5,13},{25,17},{29,21},{2,10},{... | collective-permute-start | bytes 393224 | tf_op jit(solution)/shard_map/ppermute | solution.py:209
  52.1 5.0 %collective-permute-start.8 = (f32[64,512]{1,0:T(8,128)S(1)}, f32[64,512]{1,0:T(8,128)S(1)}, u32[]{:S(2)}, u32[]{:S(2)}) collective-permute-start(f32[64,512]{1,0:T(8,128)S(1)} %collective-permute-done.7), channel_id=1, source_target_pairs={{0,1},{1,0},{2,3},{3,2},{4,5},{5,4},{6,7},{7,6},{8,9},{9,8},{10,11... | collective-permute-start | bytes 393224 | tf_op jit(solution)/shard_map/ppermute | solution.py:210
  57.1 34.9 %collective-permute-start.4 = (f32[256,512]{1,0:T(8,128)S(1)}, f32[256,512]{1,0:T(8,128)S(1)}, u32[]{:S(2)}, u32[]{:S(2)}) collective-permute-start(f32[256,512]{1,0:T(8,128)S(1)} %copy-done.1), channel_id=1, source_target_pairs={{0,4},{4,0},{8,12},{12,8},{16,20},{20,16},{24,28},{28,24},{1,5},{5... | collective-permute-start | bytes 1572872 | tf_op jit(solution)/shard_map/ppermute | solution.py:238
  57.6 6.7 %collective-permute-start.25 = (f32[64,512]{1,0:T(8,128)S(1)}, f32[64,512]{1,0:T(8,128)S(1)}, u32[]{:S(2)}, u32[]{:S(2)}) collective-permute-start(f32[64,512]{1,0:T(8,128)S(1)} %convolution_add_fusion.8), channel_id=1, source_target_pairs={{0,8},{4,12},{24,16},{28,20},{8,0},{12,4},{16,24},{20,28},{1,9},{5... | collective-permute-start | bytes 393224 | tf_op jit(solution)/shard_map/ppermute | solution.py:220
  61.5 19.1 %collective-permute-start.14 = (f32[248,512]{1,0:T(8,128)S(1)}, f32[248,512]{1,0:T(8,128)S(1)}, u32[]{:S(2)}, u32[]{:S(2)}) collective-permute-start(f32[248,512]{1,0:T(8,128)S(1)} %convolution_add_fusion.5), channel_id=1, source_target_pairs={{0,8},{4,12},{24,16},{28,20},{1,9},{5,13},{25,17},{29,21},{2,10},{... | collective-permute-start | bytes 1523720 | tf_op jit(solution)/shard_map/ppermute | solution.py:245
  64.4 2.3 %collective-permute-start.26 = (f32[64,512]{1,0:T(8,128)S(1)}, f32[64,512]{1,0:T(8,128)S(1)}, u32[]{:S(2)}, u32[]{:S(2)}) collective-permute-start(f32[64,512]{1,0:T(8,128)S(1)} %add.234), channel_id=1, source_target_pairs={{8,16},{12,20},{16,8},{20,12},{9,17},{13,21},{17,9},{21,13},{10,18... | collective-permute-start | bytes 393224 | tf_op jit(solution)/shard_map/ppermute | solution.py:221
  66.7 25.3 %copy-start = (f32[256,512]{1,0:T(8,128)S(1)}, f32[256,512]{1,0:T(8,128)}, u32[]{:S(2)}) copy-start(f32[256,512]{1,0:T(8,128)} %get-tuple-element.45) | copy-start | bytes 1572868
  66.7 26.0 %collective-permute-start.9 = (f32[128,512]{1,0:T(8,128)S(1)}, f32[128,512]{1,0:T(8,128)S(1)}, u32[]{:S(2)}, u32[]{:S(2)}) collective-permute-start(f32[128,512]{1,0:T(8,128)S(1)} %maximum_select_fusion.3), channel_id=1, source_target_pairs={{0,2},{1,3},{2,0},{3,1},{4,6},{5,7},{6,4},{7,5},{8,10},{9,11},{10,... | collective-permute-start | bytes 786440 | tf_op jit(solution)/shard_map/ppermute | solution.py:211
  67.3 10.5 %collective-permute-start.27 = (f32[64,512]{1,0:T(8,128)S(1)}, f32[64,512]{1,0:T(8,128)S(1)}, u32[]{:S(2)}, u32[]{:S(2)}) collective-permute-start(f32[64,512]{1,0:T(8,128)S(1)} %add.235), channel_id=1, source_target_pairs={{8,0},{12,4},{16,24},{20,28},{9,1},{13,5},{17,25},{21,29},{10,2},{... | collective-permute-start | bytes 393224 | tf_op jit(solution)/shard_map/ppermute | solution.py:222
  77.8 14.1 %collective-permute-start.17 = (f32[264,512]{1,0:T(8,128)S(1)}, f32[264,512]{1,0:T(8,128)S(1)}, u32[]{:S(2)}, u32[]{:S(2)}) collective-permute-start(f32[264,512]{1,0:T(8,128)S(1)} %convolution_add_fusion.3), channel_id=1, source_target_pairs={{0,8},{4,12},{24,16},{28,20},{1,9},{5,13},{25,17},{29,21},{2,10},{... | collective-permute-start | bytes 1622024 | tf_op jit(solution)/shard_map/ppermute | solution.py:245
  79.4 23.1 %collective-permute-start.23 = (f32[240,512]{1,0:T(8,128)S(1)}, f32[240,512]{1,0:T(8,128)S(1)}, u32[]{:S(2)}, u32[]{:S(2)}) collective-permute-start(f32[240,512]{1,0:T(8,128)S(1)} %convolution_add_fusion.7), channel_id=1, source_target_pairs={{0,8},{4,12},{24,16},{28,20},{1,9},{5,13},{25,17},{29,21},{2,10},{... | collective-permute-start | bytes 1474568 | tf_op jit(solution)/shard_map/ppermute | solution.py:245
  80.7 5.0 %collective-permute-start.28 = (f32[64,512]{1,0:T(8,128)S(1)}, f32[64,512]{1,0:T(8,128)S(1)}, u32[]{:S(2)}, u32[]{:S(2)}) collective-permute-start(f32[64,512]{1,0:T(8,128)S(1)} %broadcast_select_fusion), channel_id=1, source_target_pairs={{0,1},{1,0},{2,3},{3,2},{4,5},{5,4},{6,7},{7,6},{8,9},{9,8},{10,11... | collective-permute-start | bytes 393224 | tf_op jit(solution)/shard_map/ppermute | solution.py:224
  85.7 25.6 %collective-permute-start.21 = (f32[272,512]{1,0:T(8,128)S(1)}, f32[272,512]{1,0:T(8,128)S(1)}, u32[]{:S(2)}, u32[]{:S(2)}) collective-permute-start(f32[272,512]{1,0:T(8,128)S(1)} %convolution_add_fusion.2), channel_id=1, source_target_pairs={{0,8},{4,12},{24,16},{28,20},{1,9},{5,13},{25,17},{29,21},{2,10},{... | collective-permute-start | bytes 1671176 | tf_op jit(solution)/shard_map/ppermute | solution.py:245
  91.9 20.2 %collective-permute-start.12 = (f32[256,512]{1,0:T(8,128)S(1)}, f32[256,512]{1,0:T(8,128)S(1)}, u32[]{:S(2)}, u32[]{:S(2)}) collective-permute-start(f32[256,512]{1,0:T(8,128)S(1)} %copy-done), channel_id=1, source_target_pairs={{0,4},{4,0},{8,12},{12,8},{16,20},{20,16},{24,28},{28,24},{1,5},{5... | collective-permute-start | bytes 1572872 | tf_op jit(solution)/shard_map/ppermute | solution.py:238
  92.0 20.8 %collective-permute-start.15 = (f32[248,512]{1,0:T(8,128)S(1)}, f32[248,512]{1,0:T(8,128)S(1)}, u32[]{:S(2)}, u32[]{:S(2)}) collective-permute-start(f32[248,512]{1,0:T(8,128)S(1)} %add.215), channel_id=1, source_target_pairs={{8,16},{12,20},{16,8},{20,12},{9,17},{13,21},{17,9},{21,13},{10,18... | collective-permute-start | bytes 1523720 | tf_op jit(solution)/shard_map/ppermute | solution.py:245
  92.7 18.7 %collective-permute-start.29 = (f32[128,512]{1,0:T(8,128)S(1)}, f32[128,512]{1,0:T(8,128)S(1)}, u32[]{:S(2)}, u32[]{:S(2)}) collective-permute-start(f32[128,512]{1,0:T(8,128)S(1)} %maximum_select_fusion.4), channel_id=1, source_target_pairs={{0,2},{1,3},{2,0},{3,1},{4,6},{5,7},{6,4},{7,5},{8,10},{9,11},{10,... | collective-permute-start | bytes 786440 | tf_op jit(solution)/shard_map/ppermute | solution.py:225
  102.5 11.5 %collective-permute-start.18 = (f32[264,512]{1,0:T(8,128)S(1)}, f32[264,512]{1,0:T(8,128)S(1)}, u32[]{:S(2)}, u32[]{:S(2)}) collective-permute-start(f32[264,512]{1,0:T(8,128)S(1)} %add.219), channel_id=1, source_target_pairs={{8,16},{12,20},{16,8},{20,12},{9,17},{13,21},{17,9},{21,13},{10,18... | collective-permute-start | bytes 1622024 | tf_op jit(solution)/shard_map/ppermute | solution.py:245
  111.4 3.3 %collective-permute-start.10 = (f32[256,512]{1,0:T(8,128)S(1)}, f32[256,512]{1,0:T(8,128)S(1)}, u32[]{:S(2)}, u32[]{:S(2)}) collective-permute-start(f32[256,512]{1,0:T(8,128)S(1)} %constant_dynamic-slice_fusion.3), channel_id=1, source_target_pairs={{0,4},{4,0},{8,12},{12,8},{16,20},{20,16},{24,28},{28,24},{1,5},{5... | collective-permute-start | bytes 1572872 | tf_op jit(solution)/shard_map/ppermute | solution.py:206
  111.5 4.5 %collective-permute-start.11 = (f32[256,512]{1,0:T(8,128)S(1)}, f32[256,512]{1,0:T(8,128)S(1)}, u32[]{:S(2)}, u32[]{:S(2)}) collective-permute-start(f32[256,512]{1,0:T(8,128)S(1)} %maximum_select_fusion.1), channel_id=1, source_target_pairs={{0,4},{4,0},{8,12},{12,8},{16,20},{20,16},{24,28},{28,24},{1,5},{5... | collective-permute-start | bytes 1572872 | tf_op jit(solution)/shard_map/ppermute | solution.py:212
  112.1 31.8 %collective-permute-start.24 = (f32[240,512]{1,0:T(8,128)S(1)}, f32[240,512]{1,0:T(8,128)S(1)}, u32[]{:S(2)}, u32[]{:S(2)}) collective-permute-start(f32[240,512]{1,0:T(8,128)S(1)} %add.229), channel_id=1, source_target_pairs={{8,16},{12,20},{16,8},{20,12},{9,17},{13,21},{17,9},{21,13},{10,18... | collective-permute-start | bytes 1474568 | tf_op jit(solution)/shard_map/ppermute | solution.py:245
  112.8 31.1 %collective-permute-start.22 = (f32[272,512]{1,0:T(8,128)S(1)}, f32[272,512]{1,0:T(8,128)S(1)}, u32[]{:S(2)}, u32[]{:S(2)}) collective-permute-start(f32[272,512]{1,0:T(8,128)S(1)} %add.227), channel_id=1, source_target_pairs={{8,16},{12,20},{16,8},{20,12},{9,17},{13,21},{17,9},{21,13},{10,18... | collective-permute-start | bytes 1671176 | tf_op jit(solution)/shard_map/ppermute | solution.py:245
  114.0 4.2 %collective-permute-start.30 = (f32[256,512]{1,0:T(8,128)S(1)}, f32[256,512]{1,0:T(8,128)S(1)}, u32[]{:S(2)}, u32[]{:S(2)}) collective-permute-start(f32[256,512]{1,0:T(8,128)S(1)} %maximum_select_fusion.2), channel_id=1, source_target_pairs={{0,4},{4,0},{8,12},{12,8},{16,20},{20,16},{24,28},{28,24},{1,5},{5... | collective-permute-start | bytes 1572872 | tf_op jit(solution)/shard_map/ppermute | solution.py:226
  114.7 29.3 %collective-permute-start.16 = (f32[248,512]{1,0:T(8,128)S(1)}, f32[248,512]{1,0:T(8,128)S(1)}, u32[]{:S(2)}, u32[]{:S(2)}) collective-permute-start(f32[248,512]{1,0:T(8,128)S(1)} %fusion.5), channel_id=1, source_target_pairs={{8,0},{12,4},{16,24},{20,28},{9,1},{13,5},{17,25},{21,29},{10,2},{... | collective-permute-start | bytes 1523720 | tf_op jit(solution)/shard_map/ppermute | solution.py:245
  116.0 32.2 %collective-permute-start.19 = (f32[264,512]{1,0:T(8,128)S(1)}, f32[264,512]{1,0:T(8,128)S(1)}, u32[]{:S(2)}, u32[]{:S(2)}) collective-permute-start(f32[264,512]{1,0:T(8,128)S(1)} %fusion.4), channel_id=1, source_target_pairs={{8,0},{12,4},{16,24},{20,28},{9,1},{13,5},{17,25},{21,29},{10,2},{... | collective-permute-start | bytes 1622024 | tf_op jit(solution)/shard_map/ppermute | solution.py:245
where the time goes:
time: 155 us; the launch traced here: 152 us
  waiting for transfers between devices  57.2 us (37%)
  starting transfers between devices  34.1 us (22%)
  Pallas kernels  28.2 us (18%)
  matrix products  22.3 us (14%)
  local copies, waits for them, and re-layouts  5.03 us (3%)
  other arithmetic  3.8 us (2%)
    pallas_call x4, Pallas kernels, inverse_factor(): pl.pallas_call(functools.partial(invert_step, low, low == 0), out_shape=(...  25.6 us
    ppermute x10, waiting for transfers between devices, travel(): return [lax.ppermute(value, 'grp', pairs) for value in values]  24.5 us
    dot_general x19, matrix products, dot(): lax.dot_general(left, right, (((over_left,), (over_right,)), ((), ())), p...  22.3 us
    ppermute x10, starting transfers between devices, travel(): return [lax.ppermute(value, 'grp', pairs) for value in values]  11.6 us
    ppermute x1, waiting for transfers between devices, on_line(): end = lax.ppermute(quarter, 'grp', INWARD)  10.5 us
    ppermute x1, waiting for transfers between devices, on_line(): outer = lax.ppermute(part, 'grp', OUTWARD)  8.7 us
    ppermute x1, waiting for transfers between devices, on_line(): lax.ppermute(first, 'col', x_pairs)  5.17 us
    ppermute x1, starting transfers between devices, on_line(): early = lax.ppermute(early, 'grp', INWARD)  3.55 us
  transfers between devices with their start and end apart: 31, of which 11 were waited for; matrix products, arithmetic and copies ran while one was open for 17% of the time, Pallas kernels for 17%

commit v1 on v0

--- a/solution.py
+++ b/solution.py
@@ -10,7 +10,6 @@
 BLOCK = 128
 LINE = 4
 HIGHEST = lax.Precision.HIGHEST
-HIGH = lax.Precision.HIGH
 
 
 def dot(left, right, over_left, over_right, precision=HIGHEST):
@@ -128,7 +127,7 @@
     return dot(mine, inverse_factor(block), 1, 1)
 
 
-def take_panel(index_ref, count_ref, rows_ref, shift_ref, first_ref, second_ref, held, sem):
+def take_panel(index_ref, count_ref, rows_ref, shift_ref, first_ref, second_ref, side_ref, held, sem, side_sem):
     depth, width = held.shape[0], rows_ref.shape[1]
     start = index_ref[0] * PANEL
     owner = start // width
@@ -137,6 +136,10 @@
     limit = jnp.where(mine, count_ref[lax.axis_index("grp")], 0)
     copy = pltpu.make_async_copy(rows_ref.at[:, pl.ds(pl.multiple_of(local, PANEL), PANEL)], held, sem)
     copy.start()
+    span = side_ref.shape[1]
+    side = pl.multiple_of(((lax.axis_index("grp") // 2) ^ 1) * span, span)
+    side_copy = pltpu.make_async_copy(rows_ref.at[:, pl.ds(side, span)], side_ref, side_sem)
+    side_copy.start()
     copy.wait()
     half = PANEL // 2
     live = lax.broadcasted_iota(jnp.int32, (depth, half), 0) < limit
@@ -146,6 +149,7 @@
             line = shift_ref[pl.ds(local // 128 + side * (half // 128) + q, 1), :]
             line = jnp.where(mine, line, 0.0)
             out[depth:, q * 128 : (q + 1) * 128] = jnp.broadcast_to(line, (8, 128))
+    side_copy.wait()
 
 
 def panel_halves(rows, shift, group_rows, panel_index):
@@ -154,10 +158,10 @@
     smem, vmem = pl.BlockSpec(memory_space=pltpu.SMEM), pl.BlockSpec(memory_space=pltpu.VMEM)
     return pl.pallas_call(
         take_panel,
-        out_shape=(shape, shape),
+        out_shape=(shape, shape, jax.ShapeDtypeStruct((depth, rows.shape[1] // LINE), jnp.float32)),
         in_specs=[smem, smem, pl.BlockSpec(memory_space=pl.ANY), vmem],
-        out_specs=(vmem, vmem),
-        scratch_shapes=[pltpu.VMEM((depth, PANEL), jnp.float32), pltpu.SemaphoreType.DMA(())],
+        out_specs=(vmem, vmem, vmem),
+        scratch_shapes=[pltpu.VMEM((depth, PANEL), jnp.float32)] + [pltpu.SemaphoreType.DMA(())] * 2,
         name="take_panel",
     )(panel_index, group_rows, rows, shift.reshape(-1, 128))
 
@@ -174,6 +178,21 @@
 
 def ordered(low, mine, other, axis):
     return jnp.where(low, jnp.concatenate([mine, other], axis), jnp.concatenate([other, mine], axis))
+
+
+def split(value):
+    high = lax.reduce_precision(value, 8, 7)
+    return high.astype(jnp.bfloat16), (value - high).astype(jnp.bfloat16)
+
+
+def stack_left(first, second):
+    high, low = split(jnp.concatenate([first, second], 0))
+    return jnp.concatenate([high, high, low], 0)
+
+
+def stack_right(first, second):
+    high, low = split(jnp.concatenate([first, second], 0))
+    return jnp.concatenate([high, low, high], 0)
 
 
 def hold(first, second, first_in=None, second_in=None):
@@ -191,7 +210,7 @@
     x_pairs = [(c, c ^ 1) for c in range(4)]
     y_pairs = [(c, c ^ 2) for c in range(4)]
 
-    first, second = panel_halves(rows, shift, group_rows, panel_index)
+    first, second, early = panel_halves(rows, shift, group_rows, panel_index)
     first, second = hold(first, second, lax.ppermute(first, "col", x_pairs), lax.ppermute(second, "col", y_pairs))
     first, second = hold(first, second)
     first, second = hold(first, second, lax.ppermute(first, "col", y_pairs), lax.ppermute(second, "col", x_pairs))
@@ -200,17 +219,13 @@
     panel, diag = sent[:depth], sent[depth]
     panel_other = lax.ppermute(panel, "grp", core_pairs)
 
-    early = lax.dynamic_slice_in_dim(rows, 2 * (z ^ 1) * share, 2 * share, 1)
     early = lax.ppermute(early, "grp", INWARD)
     early_other = lax.dynamic_slice_in_dim(early, (1 - core) * share, share, 1)
     early_other = lax.ppermute(early_other, "grp", core_pairs)
     early = lax.dynamic_slice_in_dim(early, core * share, share, 1)
-    quarter = lax.dynamic_slice_in_dim(panel, col * (depth // 4), depth // 4, 0)
-    end = lax.ppermute(quarter, "grp", INWARD)
-    end = ordered(col % 2 == 0, end, lax.ppermute(end, "col", x_pairs), 0)
-    end = ordered(col < 2, end, lax.ppermute(end, "col", y_pairs), 0)
+    end = lax.ppermute(panel, "grp", INWARD)
     end_other = lax.ppermute(end, "grp", core_pairs)
-    side = dot(early, end, 0, 0, HIGH) + dot(early_other, end_other, 0, 0, HIGH)
+    side = dot(stack_left(early, early_other), stack_right(end, end_other), 0, 0, None)
 
     piece = PANEL // 8
     at = (core * 4 + col) * piece
@@ -232,14 +247,13 @@
     to_end = [0, share // 2 - 8, share]
     to_hub = [0, share // 2 + 16, share]
 
+    right_stack = stack_right(panel, panel_other)
+
     def products(chip, cuts):
         here = lax.dynamic_slice_in_dim(rows, (2 * chip + core) * share, share, 1)
         there = lax.dynamic_slice_in_dim(rows, (2 * chip + 1 - core) * share, share, 1)
-        there = lax.ppermute(there, "grp", core_pairs)
-        return [
-            dot(here[:, lo:hi], panel, 0, 0, HIGH) + dot(there[:, lo:hi], panel_other, 0, 0, HIGH)
-            for lo, hi in zip(cuts[:-1], cuts[1:])
-        ]
+        left_stack = stack_left(here, lax.ppermute(there, "grp", core_pairs))
+        return [dot(left_stack[:, lo:hi], right_stack, 0, 0, None) for lo, hi in zip(cuts[:-1], cuts[1:])]
 
     def travel(values, pairs):
         return [lax.ppermute(value, "grp", pairs) for value in values]

time: 155 us -> 157 us (1.013)
  the two profiles are of different devices: /device:TPU:0 before, /device:TPU:8 now
where the time goes in v1:
time: 157 us; the launch traced here: 156 us
  waiting for transfers between devices  68.9 us (44%)
  starting transfers between devices  35.5 us (23%)
  Pallas kernels  28.9 us (18%)
  matrix products  10.6 us (7%)
  other arithmetic  6.49 us (4%)
  local copies, waits for them, and re-layouts  4.68 us (3%)
    ppermute x10, waiting for transfers between devices, travel(): return [lax.ppermute(value, 'grp', pairs) for value in values]  39.9 us
    pallas_call x4, Pallas kernels, inverse_factor(): pl.pallas_call(functools.partial(invert_step, low, low == 0), out_shape=(...  25.6 us
    ppermute x10, starting transfers between devices, travel(): return [lax.ppermute(value, 'grp', pairs) for value in values]  17.4 us
    dot_general x11, matrix products, dot(): lax.dot_general(left, right, (((over_left,), (over_right,)), ((), ())), p...  10.6 us
    ppermute x1, waiting for transfers between devices, on_line(): part = part + lax.ppermute(part, 'grp', SIDE)  10.2 us
    ppermute x1, waiting for transfers between devices, on_line(): early = lax.ppermute(early, 'grp', INWARD)  4.69 us
    ppermute x1, starting transfers between devices, on_line(): outer = lax.ppermute(part, 'grp', OUTWARD)  4.61 us
    dynamic_slice x1, local copies, waits for them, and re-layouts, products(): here = lax.dynamic_slice_in_dim(rows, (2 * chip + core) * share, share, 1)  3.77 us
  transfers between devices with their start and end apart: 29, of which 13 were waited for; matrix products, arithmetic and copies ran while one was open for 10% of the time, Pallas kernels for 18%

profile of v1, /device:TPU:8, one launch (start us, length us, event | category | flops | bytes accessed | tf_op | source)
XLA Modules:
  0.0 156.3 jit_solution(13869149048585213024)
XLA Ops:
  0.0 3.8 %constant_dynamic-slice_fusion.9 = (f32[256,512]{1,0:T(8,128)S(1)}, f32[256,512]{1,0:T(8,128)}, f32[256,512]{1,0:T(8,128)S(1)}, f32[256,512]{1,0:T(8,128)}, f32[...) fusion(f32[256,4096]{1,0:T(8,128)} %rows_ref.1, s32[]{:T(128)S(6)} %select_n.101, ...), kind=kLoop, calls=%fused_computation.104 | loop fusion | bytes 8388640 | tf_op jit(solution)/shard_map/dynamic_slice | solution.py:253
  4.9 3.3 %take_panel.1 = (f32[264,256]{1,0:T(8,128)}, f32[264,256]{1,0:T(8,128)}, f32[256,1024]{1,0:T(8,128)}) custom-call(s32[1]{0:T(128)S(6)} %copy.6.index_ref, s32[8]{0:T(128)} %count_ref.1, f32[256,4096]{1,0:T(8,128)} %rows_ref.1, f32[32,128]{1,0:T(8,128)} %bitcast.6), custom_call_target="tpu_custom_call" | custom-call | tf_op jit(solution)/shard_map/take_panel/pallas_call | solution.py:159
  8.2 1.6 collective-permute-start.1
  9.8 1.5 collective-permute-start.2
  11.3 1.3 collective-permute-start.6
  12.7 0.8 dynamic_slice.43
  13.4 3.5 %collective-permute-done.1 = f32[264,256]{1,0:T(8,128)S(1)} collective-permute-done((f32[264,256]{1,0:T(8,128)}, f32[264,256]{1,0:T(8,128)S(1)}, u32[]{:S(2)}, u32[]{:S(2)}) %collective-permute-start.1) | collective-permute-done | bytes 270368 | tf_op jit(solution)/shard_map/ppermute | solution.py:214
  16.9 1.3 collective-permute-done.2
  18.2 1.0 add.155
  19.2 1.1 add.156
  20.3 1.6 %collective-permute-start.3 = (f32[264,256]{1,0:T(8,128)S(1)}, f32[264,256]{1,0:T(8,128)S(1)}, u32[]{:S(2)}, u32[]{:S(2)}) collective-permute-start(f32[264,256]{1,0:T(8,128)S(1)} %add.155), channel_id=1, source_target_pairs={{0,2},{1,3},{2,0},{3,1},{4,6},{5,7},{6,4},{7,5},{8,10},{9,11},{10,... | collective-permute-start | bytes 811016 | tf_op jit(solution)/shard_map/ppermute | solution.py:216
  21.9 1.2 reduce-precision_convert_fusion.1
  23.1 0.8 collective-permute-start.4
  23.9 1.2 reduce-precision_convert_fusion.2
  25.6 3.6 %collective-permute-done.3 = f32[264,256]{1,0:T(8,128)S(1)} collective-permute-done((f32[264,256]{1,0:T(8,128)S(1)}, f32[264,256]{1,0:T(8,128)S(1)}, u32[]{:S(2)}, u32[]{:S(2)}) %collective-permute-start.3) | collective-permute-done | bytes 270368 | tf_op jit(solution)/shard_map/ppermute | solution.py:216
  29.3 2.5 %collective-permute-done.4 = f32[264,256]{1,0:T(8,128)S(1)} collective-permute-done((f32[264,256]{1,0:T(8,128)S(1)}, f32[264,256]{1,0:T(8,128)S(1)}, u32[]{:S(2)}, u32[]{:S(2)}) %collective-permute-start.4) | collective-permute-done | bytes 270368 | tf_op jit(solution)/shard_map/ppermute | solution.py:216
  32.2 1.3 collective-permute-start.8
  34.0 4.7 %collective-permute-done.6 = f32[256,1024]{1,0:T(8,128)S(1)} collective-permute-done((f32[256,1024]{1,0:T(8,128)}, f32[256,1024]{1,0:T(8,128)S(1)}, u32[]{:S(2)}, u32[]{:S(2)}) %collective-permute-start.6) | collective-permute-done | bytes 1048608 | tf_op jit(solution)/shard_map/ppermute | solution.py:222
  39.5 1.0 fusion.19
  41.7 10.2 %collective-permute-done.23 = f32[64,512]{1,0:T(8,128)S(1)} collective-permute-done((f32[64,512]{1,0:T(8,128)S(1)}, f32[64,512]{1,0:T(8,128)S(1)}, u32[]{:S(2)}, u32[]{:S(2)}) %collective-permute-start.23) | collective-permute-done | bytes 131104 | tf_op jit(solution)/shard_map/ppermute | solution.py:235
  52.0 3.5 %collective-permute-start.24 = (f32[64,512]{1,0:T(8,128)S(1)}, f32[64,512]{1,0:T(8,128)S(1)}, u32[]{:S(2)}, u32[]{:S(2)}) collective-permute-start(f32[64,512]{1,0:T(8,128)S(1)} %add.193), channel_id=1, source_target_pairs={{8,16},{12,20},{16,8},{20,12},{9,17},{13,21},{17,9},{21,13},{10,18... | collective-permute-start | bytes 393224 | tf_op jit(solution)/shard_map/ppermute | solution.py:236
  55.5 0.9 fusion.46
  56.4 1.3 collective-permute-start.12
  57.7 1.3 collective-permute-start.21
  59.0 4.6 %collective-permute-start.25 = (f32[64,512]{1,0:T(8,128)S(1)}, f32[64,512]{1,0:T(8,128)S(1)}, u32[]{:S(2)}, u32[]{:S(2)}) collective-permute-start(f32[64,512]{1,0:T(8,128)S(1)} %add.194), channel_id=1, source_target_pairs={{8,0},{12,4},{16,24},{20,28},{9,1},{13,5},{17,25},{21,29},{10,2},{... | collective-permute-start | bytes 393224 | tf_op jit(solution)/shard_map/ppermute | solution.py:237
  63.6 1.0 fusion
  64.8 1.4 collective-permute-done.25
  66.1 1.3 collective-permute-start.15
  67.4 15.8 %collective-permute-done.21 = f32[240,512]{1,0:T(8,128)S(1)} collective-permute-done((f32[240,512]{1,0:T(8,128)S(1)}, f32[240,512]{1,0:T(8,128)S(1)}, u32[]{:S(2)}, u32[]{:S(2)}) %collective-permute-start.21) | collective-permute-done | bytes 491552 | tf_op jit(solution)/shard_map/ppermute | solution.py:259
  83.2 1.3 collective-permute-start.19
  85.4 2.4 %collective-permute-start.22 = (f32[240,512]{1,0:T(8,128)S(1)}, f32[240,512]{1,0:T(8,128)S(1)}, u32[]{:S(2)}, u32[]{:S(2)}) collective-permute-start(f32[240,512]{1,0:T(8,128)S(1)} %add.187), channel_id=1, source_target_pairs={{8,16},{12,20},{16,8},{20,12},{9,17},{13,21},{17,9},{21,13},{10,18... | collective-permute-start | bytes 1474568 | tf_op jit(solution)/shard_map/ppermute | solution.py:259
  87.9 1.8 %collective-permute-done.26 = f32[64,512]{1,0:T(8,128)S(1)} collective-permute-done((f32[64,512]{1,0:T(8,128)S(1)}, f32[64,512]{1,0:T(8,128)S(1)}, u32[]{:S(2)}, u32[]{:S(2)}) %collective-permute-start.26) | collective-permute-done | bytes 131104 | tf_op jit(solution)/shard_map/ppermute | solution.py:239
  89.7 2.3 %collective-permute-start.13 = (f32[248,512]{1,0:T(8,128)S(1)}, f32[248,512]{1,0:T(8,128)S(1)}, u32[]{:S(2)}, u32[]{:S(2)}) collective-permute-start(f32[248,512]{1,0:T(8,128)S(1)} %add.177), channel_id=1, source_target_pairs={{8,16},{12,20},{16,8},{20,12},{9,17},{13,21},{17,9},{21,13},{10,18... | collective-permute-start | bytes 1523720 | tf_op jit(solution)/shard_map/ppermute | solution.py:259
  92.7 2.2 %collective-permute-done.15 = f32[264,512]{1,0:T(8,128)S(1)} collective-permute-done((f32[264,512]{1,0:T(8,128)S(1)}, f32[264,512]{1,0:T(8,128)S(1)}, u32[]{:S(2)}, u32[]{:S(2)}) %collective-permute-start.15) | collective-permute-done | bytes 540704 | tf_op jit(solution)/shard_map/ppermute | solution.py:259
  94.9 2.4 %collective-permute-start.16 = (f32[264,512]{1,0:T(8,128)S(1)}, f32[264,512]{1,0:T(8,128)S(1)}, u32[]{:S(2)}, u32[]{:S(2)}) collective-permute-start(f32[264,512]{1,0:T(8,128)S(1)} %add.179), channel_id=1, source_target_pairs={{8,16},{12,20},{16,8},{20,12},{9,17},{13,21},{17,9},{21,13},{10,18... | collective-permute-start | bytes 1622024 | tf_op jit(solution)/shard_map/ppermute | solution.py:259
  97.4 7.4 %collective-permute-done.19 = f32[272,512]{1,0:T(8,128)S(1)} collective-permute-done((f32[272,512]{1,0:T(8,128)S(1)}, f32[272,512]{1,0:T(8,128)S(1)}, u32[]{:S(2)}, u32[]{:S(2)}) %collective-permute-start.19) | collective-permute-done | bytes 557088 | tf_op jit(solution)/shard_map/ppermute | solution.py:259
  105.0 2.4 %collective-permute-start.20 = (f32[272,512]{1,0:T(8,128)S(1)}, f32[272,512]{1,0:T(8,128)S(1)}, u32[]{:S(2)}, u32[]{:S(2)}) collective-permute-start(f32[272,512]{1,0:T(8,128)S(1)} %add.186), channel_id=1, source_target_pairs={{8,16},{12,20},{16,8},{20,12},{9,17},{13,21},{17,9},{21,13},{10,18... | collective-permute-start | bytes 1671176 | tf_op jit(solution)/shard_map/ppermute | solution.py:259
  107.5 4.8 %collective-permute-done.13 = f32[248,512]{1,0:T(8,128)S(1)} collective-permute-done((f32[248,512]{1,0:T(8,128)S(1)}, f32[248,512]{1,0:T(8,128)S(1)}, u32[]{:S(2)}, u32[]{:S(2)}) %collective-permute-start.13) | collective-permute-done | bytes 507936 | tf_op jit(solution)/shard_map/ppermute | solution.py:259
  112.9 1.3 collective-permute-start.14
  114.2 9.7 %collective-permute-done.16 = f32[264,512]{1,0:T(8,128)S(1)} collective-permute-done((f32[264,512]{1,0:T(8,128)S(1)}, f32[264,512]{1,0:T(8,128)S(1)}, u32[]{:S(2)}, u32[]{:S(2)}) %collective-permute-start.16) | collective-permute-done | bytes 540704 | tf_op jit(solution)/shard_map/ppermute | solution.py:259
  123.9 1.0 fusion.23
  124.9 1.5 collective-permute-start.17
  126.4 1.0 fusion.6
  127.6 6.5 %invert_step.4 = (f32[512,512]{1,0:T(8,128)S(1)}, f32[512,512]{1,0:T(8,128)S(1)}) custom-call(f32[512,512]{1,0:T(8,128)S(1)} %fusion.41.a_in.w_in, f32[512,512]{1,0:T(8,128)S(1)} %fusion.41.a_in.w_in), custom_call_target="tpu_custom_call" | custom-call | flops 134217728 | bytes 20971520 | tf_op jit(solution)/shard_map/invert_step/pallas_call | solution.py:97
  134.1 6.4 %invert_step.5 = (f32[512,512]{1,0:T(8,128)S(1)}, f32[512,512]{1,0:T(8,128)S(1)}) custom-call(f32[512,512]{1,0:T(8,128)S(1)} %get-tuple-element.38.a_in, f32[512,512]{1,0:T(8,128)S(1)} %get-tuple-element.39.w_in), custom_call_target="tpu_custom_call" | custom-call | flops 134217728 | bytes 20971520 | tf_op jit(solution)/shard_map/invert_step/pallas_call | solution.py:97
  140.6 6.4 %invert_step.6 = (f32[512,512]{1,0:T(8,128)S(1)}, f32[512,512]{1,0:T(8,128)S(1)}) custom-call(f32[512,512]{1,0:T(8,128)S(1)} %get-tuple-element.40.a_in, f32[512,512]{1,0:T(8,128)S(1)} %get-tuple-element.41.w_in), custom_call_target="tpu_custom_call" | custom-call | flops 134217728 | bytes 20971520 | tf_op jit(solution)/shard_map/invert_step/pallas_call | solution.py:97
  147.0 6.2 %invert_step.7 = (f32[512,512]{1,0:T(8,128)}, f32[512,512]{1,0:T(8,128)S(1)}) custom-call(f32[512,512]{1,0:T(8,128)S(1)} %get-tuple-element.42.a_in, f32[512,512]{1,0:T(8,128)S(1)} %get-tuple-element.43.w_in), custom_call_target="tpu_custom_call" | custom-call | flops 134217728 | bytes 20971520 | tf_op jit(solution)/shard_map/invert_step/pallas_call | solution.py:97
  153.2 3.0 %fusion.34 = f32[512,512]{1,0:T(8,128)} fusion(f32[512,512]{1,0:T(8,128)S(1)} %get-tuple-element.44, f32[264,512]{1,0:T(8,128)S(1)} %collective-permute-done.17, f32[248,512]{1,0:T(8,128)S(1)} %collective-permute-done.14, f32[240,512]{1,0:T(8,128)S(1)} %collective-permute-done.22, f32[272,512]{1,0:T(8,128)S(1)} %collective-permute-done.20, ...), kind=kOutput, calls=%fused_computation.57 | convolution fusion | flops 1612709888 | bytes 6297600 | tf_op jit(solution)/shard_map/dot_general | solution.py:16
  (58 shorter events, 7.0 us)
Async XLA Ops:
  3.8 16.5 %collective-permute-start.11 = (f32[256,512]{1,0:T(8,128)}, f32[256,512]{1,0:T(8,128)}, u32[]{:S(2)}, u32[]{:S(2)}) collective-permute-start(f32[256,512]{1,0:T(8,128)} %get-tuple-element.46), channel_id=1, source_target_pairs={{0,4},{4,0},{8,12},{12,8},{16,20},{20,16},{24,28},{28,24},{1,5},{5... | collective-permute-start | bytes 1572872 | tf_op jit(solution)/shard_map/ppermute | solution.py:255
  3.8 19.3 %collective-permute-start.10 = (f32[256,512]{1,0:T(8,128)}, f32[256,512]{1,0:T(8,128)}, u32[]{:S(2)}, u32[]{:S(2)}) collective-permute-start(f32[256,512]{1,0:T(8,128)} %get-tuple-element.48), channel_id=1, source_target_pairs={{0,4},{4,0},{8,12},{12,8},{16,20},{20,16},{24,28},{28,24},{1,5},{5... | collective-permute-start | bytes 1572872 | tf_op jit(solution)/shard_map/ppermute | solution.py:255
  8.2 8.7 %collective-permute-start.1 = (f32[264,256]{1,0:T(8,128)}, f32[264,256]{1,0:T(8,128)S(1)}, u32[]{:S(2)}, u32[]{:S(2)}) collective-permute-start(f32[264,256]{1,0:T(8,128)} %get-tuple-element.27), channel_id=1, source_target_pairs={{0,1},{1,0},{2,3},{3,2},{4,5},{5,4},{6,7},{7,6},{8,9},{9,8},{10,11... | collective-permute-start | bytes 811016 | tf_op jit(solution)/shard_map/ppermute | solution.py:214
  9.8 8.4 %collective-permute-start.2 = (f32[264,256]{1,0:T(8,128)}, f32[264,256]{1,0:T(8,128)}, u32[]{:S(2)}, u32[]{:S(2)}) collective-permute-start(f32[264,256]{1,0:T(8,128)} %get-tuple-element.29), channel_id=1, source_target_pairs={{0,2},{1,3},{2,0},{3,1},{4,6},{5,7},{6,4},{7,5},{8,10},{9,11},{10,... | collective-permute-start | bytes 811016 | tf_op jit(solution)/shard_map/ppermute | solution.py:214
  11.3 27.3 %collective-permute-start.6 = (f32[256,1024]{1,0:T(8,128)}, f32[256,1024]{1,0:T(8,128)S(1)}, u32[]{:S(2)}, u32[]{:S(2)}) collective-permute-start(f32[256,1024]{1,0:T(8,128)} %get-tuple-element.37), channel_id=1, source_target_pairs={{0,8},{4,12},{24,16},{28,20},{1,9},{5,13},{25,17},{29,21},{2,10},{... | collective-permute-start | bytes 3145736 | tf_op jit(solution)/shard_map/ppermute | solution.py:222
  16.9 15.1 %collective-permute-start = (f32[256,512]{1,0:T(8,128)}, f32[256,512]{1,0:T(8,128)S(1)}, u32[]{:S(2)}, u32[]{:S(2)}) collective-permute-start(f32[256,512]{1,0:T(8,128)} %get-tuple-element.50), channel_id=1, source_target_pairs={{0,4},{4,0},{8,12},{12,8},{16,20},{20,16},{24,28},{28,24},{1,5},{5... | collective-permute-start | bytes 1572872 | tf_op jit(solution)/shard_map/ppermute | solution.py:255
  18.2 7.1 %collective-permute-start.18 = (f32[256,512]{1,0:T(8,128)}, f32[256,512]{1,0:T(8,128)S(1)}, u32[]{:S(2)}, u32[]{:S(2)}) collective-permute-start(f32[256,512]{1,0:T(8,128)} %get-tuple-element.51), channel_id=1, source_target_pairs={{0,4},{4,0},{8,12},{12,8},{16,20},{20,16},{24,28},{28,24},{1,5},{5... | collective-permute-start | bytes 1572872 | tf_op jit(solution)/shard_map/ppermute | solution.py:255
  20.3 9.0 %collective-permute-start.3 = (f32[264,256]{1,0:T(8,128)S(1)}, f32[264,256]{1,0:T(8,128)S(1)}, u32[]{:S(2)}, u32[]{:S(2)}) collective-permute-start(f32[264,256]{1,0:T(8,128)S(1)} %add.155), channel_id=1, source_target_pairs={{0,2},{1,3},{2,0},{3,1},{4,6},{5,7},{6,4},{7,5},{8,10},{9,11},{10,... | collective-permute-start | bytes 811016 | tf_op jit(solution)/shard_map/ppermute | solution.py:216
  23.1 8.7 %collective-permute-start.4 = (f32[264,256]{1,0:T(8,128)S(1)}, f32[264,256]{1,0:T(8,128)S(1)}, u32[]{:S(2)}, u32[]{:S(2)}) collective-permute-start(f32[264,256]{1,0:T(8,128)S(1)} %add.156), channel_id=1, source_target_pairs={{0,1},{1,0},{2,3},{3,2},{4,5},{5,4},{6,7},{7,6},{8,9},{9,8},{10,11... | collective-permute-start | bytes 811016 | tf_op jit(solution)/shard_map/ppermute | solution.py:216
  31.9 6.9 %collective-permute-start.5 = (f32[256,512]{1,0:T(8,128)S(1)}, f32[256,512]{1,0:T(8,128)S(1)}, u32[]{:S(2)}, u32[]{:S(2)}) collective-permute-start(f32[256,512]{1,0:T(8,128)S(1)} %fusion.55), channel_id=1, source_target_pairs={{0,4},{4,0},{8,12},{12,8},{16,20},{20,16},{24,28},{28,24},{1,5},{5... | collective-permute-start | bytes 1572872 | tf_op jit(solution)/shard_map/ppermute | solution.py:220
  32.2 32.4 %collective-permute-start.8 = (f32[256,512]{1,0:T(8,128)S(1)}, f32[256,512]{1,0:T(8,128)S(1)}, u32[]{:S(2)}, u32[]{:S(2)}) collective-permute-start(f32[256,512]{1,0:T(8,128)S(1)} %fusion.55), channel_id=1, source_target_pairs={{0,8},{4,12},{24,16},{28,20},{1,9},{5,13},{25,17},{29,21},{2,10},{... | collective-permute-start | bytes 1572872 | tf_op jit(solution)/shard_map/ppermute | solution.py:226
  38.7 45.9 %collective-permute-start.7 = (f32[256,512]{1,0:T(8,128)S(1)}, f32[256,512]{1,0:T(8,128)S(1)}, u32[]{:S(2)}, u32[]{:S(2)}) collective-permute-start(f32[256,512]{1,0:T(8,128)S(1)} %get-tuple-element.58), channel_id=1, source_target_pairs={{0,4},{4,0},{8,12},{12,8},{16,20},{20,16},{24,28},{28,24},{1,5},{5... | collective-permute-start | bytes 1572872 | tf_op jit(solution)/shard_map/ppermute | solution.py:224
  39.3 12.7 %collective-permute-start.23 = (f32[64,512]{1,0:T(8,128)S(1)}, f32[64,512]{1,0:T(8,128)S(1)}, u32[]{:S(2)}, u32[]{:S(2)}) collective-permute-start(f32[64,512]{1,0:T(8,128)S(1)} %convolution_add_fusion), channel_id=1, source_target_pairs={{0,8},{4,12},{24,16},{28,20},{8,0},{12,4},{16,24},{20,28},{1,9},{5... | collective-permute-start | bytes 393224 | tf_op jit(solution)/shard_map/ppermute | solution.py:235
  52.0 7.0 %collective-permute-start.24 = (f32[64,512]{1,0:T(8,128)S(1)}, f32[64,512]{1,0:T(8,128)S(1)}, u32[]{:S(2)}, u32[]{:S(2)}) collective-permute-start(f32[64,512]{1,0:T(8,128)S(1)} %add.193), channel_id=1, source_target_pairs={{8,16},{12,20},{16,8},{20,12},{9,17},{13,21},{17,9},{21,13},{10,18... | collective-permute-start | bytes 393224 | tf_op jit(solution)/shard_map/ppermute | solution.py:236
  56.4 29.0 %collective-permute-start.12 = (f32[248,512]{1,0:T(8,128)S(1)}, f32[248,512]{1,0:T(8,128)S(1)}, u32[]{:S(2)}, u32[]{:S(2)}) collective-permute-start(f32[248,512]{1,0:T(8,128)S(1)} %fusion.48), channel_id=1, source_target_pairs={{0,8},{4,12},{24,16},{28,20},{1,9},{5,13},{25,17},{29,21},{2,10},{... | collective-permute-start | bytes 1523720 | tf_op jit(solution)/shard_map/ppermute | solution.py:259
  57.7 25.6 %collective-permute-start.21 = (f32[240,512]{1,0:T(8,128)S(1)}, f32[240,512]{1,0:T(8,128)S(1)}, u32[]{:S(2)}, u32[]{:S(2)}) collective-permute-start(f32[240,512]{1,0:T(8,128)S(1)} %fusion.46), channel_id=1, source_target_pairs={{0,8},{4,12},{24,16},{28,20},{1,9},{5,13},{25,17},{29,21},{2,10},{... | collective-permute-start | bytes 1474568 | tf_op jit(solution)/shard_map/ppermute | solution.py:259
  59.0 7.1 %collective-permute-start.25 = (f32[64,512]{1,0:T(8,128)S(1)}, f32[64,512]{1,0:T(8,128)S(1)}, u32[]{:S(2)}, u32[]{:S(2)}) collective-permute-start(f32[64,512]{1,0:T(8,128)S(1)} %add.194), channel_id=1, source_target_pairs={{8,0},{12,4},{16,24},{20,28},{9,1},{13,5},{17,25},{21,29},{10,2},{... | collective-permute-start | bytes 393224 | tf_op jit(solution)/shard_map/ppermute | solution.py:237
  64.6 27.4 %collective-permute-start.9 = (f32[256,512]{1,0:T(8,128)S(1)}, f32[256,512]{1,0:T(8,128)S(1)}, u32[]{:S(2)}, u32[]{:S(2)}) collective-permute-start(f32[256,512]{1,0:T(8,128)S(1)} %collective-permute-done.8), channel_id=1, source_target_pairs={{0,4},{4,0},{8,12},{12,8},{16,20},{20,16},{24,28},{28,24},{1,5},{5... | collective-permute-start | bytes 1572872 | tf_op jit(solution)/shard_map/ppermute | solution.py:227
  66.1 28.7 %collective-permute-start.15 = (f32[264,512]{1,0:T(8,128)S(1)}, f32[264,512]{1,0:T(8,128)S(1)}, u32[]{:S(2)}, u32[]{:S(2)}) collective-permute-start(f32[264,512]{1,0:T(8,128)S(1)} %fusion.19), channel_id=1, source_target_pairs={{0,8},{4,12},{24,16},{28,20},{1,9},{5,13},{25,17},{29,21},{2,10},{... | collective-permute-start | bytes 1622024 | tf_op jit(solution)/shard_map/ppermute | solution.py:259
  83.2 21.6 %collective-permute-start.19 = (f32[272,512]{1,0:T(8,128)S(1)}, f32[272,512]{1,0:T(8,128)S(1)}, u32[]{:S(2)}, u32[]{:S(2)}) collective-permute-start(f32[272,512]{1,0:T(8,128)S(1)} %fusion.17), channel_id=1, source_target_pairs={{0,8},{4,12},{24,16},{28,20},{1,9},{5,13},{25,17},{29,21},{2,10},{... | collective-permute-start | bytes 1671176 | tf_op jit(solution)/shard_map/ppermute | solution.py:259
  84.6 5.0 %collective-permute-start.26 = (f32[64,512]{1,0:T(8,128)S(1)}, f32[64,512]{1,0:T(8,128)S(1)}, u32[]{:S(2)}, u32[]{:S(2)}) collective-permute-start(f32[64,512]{1,0:T(8,128)S(1)} %broadcast_select_fusion), channel_id=1, source_target_pairs={{0,1},{1,0},{2,3},{3,2},{4,5},{5,4},{6,7},{7,6},{8,9},{9,8},{10,11... | collective-permute-start | bytes 393224 | tf_op jit(solution)/shard_map/ppermute | solution.py:239
  85.4 67.8 %collective-permute-start.22 = (f32[240,512]{1,0:T(8,128)S(1)}, f32[240,512]{1,0:T(8,128)S(1)}, u32[]{:S(2)}, u32[]{:S(2)}) collective-permute-start(f32[240,512]{1,0:T(8,128)S(1)} %add.187), channel_id=1, source_target_pairs={{8,16},{12,20},{16,8},{20,12},{9,17},{13,21},{17,9},{21,13},{10,18... | collective-permute-start | bytes 1474568 | tf_op jit(solution)/shard_map/ppermute | solution.py:259
  89.7 22.6 %collective-permute-start.13 = (f32[248,512]{1,0:T(8,128)S(1)}, f32[248,512]{1,0:T(8,128)S(1)}, u32[]{:S(2)}, u32[]{:S(2)}) collective-permute-start(f32[248,512]{1,0:T(8,128)S(1)} %add.177), channel_id=1, source_target_pairs={{8,16},{12,20},{16,8},{20,12},{9,17},{13,21},{17,9},{21,13},{10,18... | collective-permute-start | bytes 1523720 | tf_op jit(solution)/shard_map/ppermute | solution.py:259
  92.0 15.3 %collective-permute-start.27 = (f32[128,512]{1,0:T(8,128)S(1)}, f32[128,512]{1,0:T(8,128)S(1)}, u32[]{:S(2)}, u32[]{:S(2)}) collective-permute-start(f32[128,512]{1,0:T(8,128)S(1)} %maximum_select_fusion.2), channel_id=1, source_target_pairs={{0,2},{1,3},{2,0},{3,1},{4,6},{5,7},{6,4},{7,5},{8,10},{9,11},{10,... | collective-permute-start | bytes 786440 | tf_op jit(solution)/shard_map/ppermute | solution.py:240
  94.9 28.9 %collective-permute-start.16 = (f32[264,512]{1,0:T(8,128)S(1)}, f32[264,512]{1,0:T(8,128)S(1)}, u32[]{:S(2)}, u32[]{:S(2)}) collective-permute-start(f32[264,512]{1,0:T(8,128)S(1)} %add.179), channel_id=1, source_target_pairs={{8,16},{12,20},{16,8},{20,12},{9,17},{13,21},{17,9},{21,13},{10,18... | collective-permute-start | bytes 1622024 | tf_op jit(solution)/shard_map/ppermute | solution.py:259
  105.0 48.2 %collective-permute-start.20 = (f32[272,512]{1,0:T(8,128)S(1)}, f32[272,512]{1,0:T(8,128)S(1)}, u32[]{:S(2)}, u32[]{:S(2)}) collective-permute-start(f32[272,512]{1,0:T(8,128)S(1)} %add.186), channel_id=1, source_target_pairs={{8,16},{12,20},{16,8},{20,12},{9,17},{13,21},{17,9},{21,13},{10,18... | collective-permute-start | bytes 1671176 | tf_op jit(solution)/shard_map/ppermute | solution.py:259
  107.4 20.0 %collective-permute-start.28 = (f32[256,512]{1,0:T(8,128)S(1)}, f32[256,512]{1,0:T(8,128)S(1)}, u32[]{:S(2)}, u32[]{:S(2)}) collective-permute-start(f32[256,512]{1,0:T(8,128)S(1)} %maximum_select_fusion.1), channel_id=1, source_target_pairs={{0,4},{4,0},{8,12},{12,8},{16,20},{20,16},{24,28},{28,24},{1,5},{5... | collective-permute-start | bytes 1572872 | tf_op jit(solution)/shard_map/ppermute | solution.py:241
  112.9 40.4 %collective-permute-start.14 = (f32[248,512]{1,0:T(8,128)S(1)}, f32[248,512]{1,0:T(8,128)S(1)}, u32[]{:S(2)}, u32[]{:S(2)}) collective-permute-start(f32[248,512]{1,0:T(8,128)S(1)} %fusion.52), channel_id=1, source_target_pairs={{8,0},{12,4},{16,24},{20,28},{9,1},{13,5},{17,25},{21,29},{10,2},{... | collective-permute-start | bytes 1523720 | tf_op jit(solution)/shard_map/ppermute | solution.py:259
  124.9 28.4 %collective-permute-start.17 = (f32[264,512]{1,0:T(8,128)S(1)}, f32[264,512]{1,0:T(8,128)S(1)}, u32[]{:S(2)}, u32[]{:S(2)}) collective-permute-start(f32[264,512]{1,0:T(8,128)S(1)} %fusion.23), channel_id=1, source_target_pairs={{8,0},{12,4},{16,24},{20,28},{9,1},{13,5},{17,25},{21,29},{10,2},{... | collective-permute-start | bytes 1622024 | tf_op jit(solution)/shard_map/ppermute | solution.py:259
